TPU v7x, 256 devices: a whole 4x4x8 slice. The times are simulated.
256 devices in a mesh: leaf: 32 (over x_hi, z, core), head: 8 (over x_lo, y).
Axes of the slice: x: 4 (x_hi: 2, x_lo: 2; x = x_hi * 2 + x_lo), y: 4, z: 8, core: 2. Of those that a mesh axis runs over, the one named last changes fastest.
Arguments:
- latents: bfloat16 [2048, 512], P('leaf'), may hold values from -14 to 14
- queries: bfloat16 [4096, 64, 128], P('leaf', 'head'), may hold values from -14 to 14
- grad_out: bfloat16 [4096, 64, 128], P('leaf', 'head'), may hold values from -6 to 6
- key_up_matrix: bfloat16 [64, 128, 512], P('head'), may hold values from -0.25 to 0.25
- value_up_matrix: bfloat16 [64, 512, 128], P('head'), may hold values from -0.25 to 0.25
- parents: int32 [256], replicated, may hold values from 0 to 254, as said below
- branch_node: int32 [32, 8], P('leaf'), may hold values from 0 to 255
- branch_lengths: int32 [32, 8], P('leaf'), may hold values from 1 to 40, 128 in all within a row
Outputs:
- d_queries: bfloat16 [4096, 64, 128], P('leaf', 'head')
- d_latents: float32 [2048, 512], P('leaf')
Inputs may be any that keep to these rules, and one draw needn't show every extreme that they name: parents[0] = 0 and parents[n] < n for every n >= 1.
All inputs are finite; a program needn't handle non-finite values.
Results may differ from a plain program's by a relative error of at most 0.025.
The roundings to bfloat16 on the way count: a program that leaves them out, or rounds other values in their place, can miss the bound.
Values may be sent and summed in bfloat16 or wider, within the bound.
A program may use at most 64 MiB of HBM per device.

v0:
```python
import jax
import jax.numpy as jnp
from jax import lax
from jax.sharding import PartitionSpec as P

NODE_LEN = 8
softmax_scale = 192.0 ** (-0.5)
masked_score = -1e30


def ancestry(parents):
    node_count = parents.shape[0]
    indices = jnp.arange(node_count, dtype=jnp.int32)
    linked = (parents[:, None] == indices[None, :]) | (indices[:, None] == indices[None, :])
    closure = linked.astype(jnp.float32)
    for squaring in range(node_count.bit_length()):
        closure = jnp.minimum(jnp.dot(closure, closure, precision=lax.Precision.HIGHEST), 1.0)
    return closure


def token_nodes(lengths_row, nodes_row, tok_count):
    bounds = jnp.cumsum(lengths_row)
    places = jnp.arange(tok_count, dtype=jnp.int32)
    branch_of = jnp.sum((places[:, None] >= bounds[None, :]).astype(jnp.int32), axis=1)
    select = branch_of[:, None] == jnp.arange(lengths_row.shape[0], dtype=jnp.int32)[None, :]
    return jnp.sum(jnp.where(select, nodes_row[None, :], 0), axis=1)


def live_keys(node_list, closure):
    node_count = closure.shape[0]
    select = (node_list[:, None] == jnp.arange(node_count, dtype=jnp.int32)[None, :]).astype(
        jnp.float32
    )
    reached = jnp.dot(select, closure, precision=lax.Precision.HIGHEST) > 0.5
    return jnp.repeat(reached, NODE_LEN, axis=1)


def on_device(
    latents, queries, grad_out, key_up_matrix, value_up_matrix, parents, branch_node, branch_lengths
):
    closure = ancestry(parents)
    tok_count = queries.shape[0]
    heads_here = queries.shape[1]
    width = latents.shape[1]
    node_list = token_nodes(branch_lengths[0], branch_node[0], tok_count)
    key_live = live_keys(node_list, closure)
    prefix_rows = key_live.shape[1]
    query_latent = jnp.einsum(
        "thd,hdc->thc", queries, key_up_matrix, preferred_element_type=jnp.float32
    ).astype(jnp.bfloat16)
    grad_latent = jnp.einsum(
        "thv,hcv->thc", grad_out, value_up_matrix, preferred_element_type=jnp.float32
    ).astype(jnp.bfloat16)

    def scores(block_keys):
        usable = key_live[:, None, :]
        scaled = (
            jnp.einsum("thc,kc->thk", query_latent, block_keys, preferred_element_type=jnp.float32)
            * softmax_scale
        )
        return (usable, jnp.where(usable, scaled, masked_score))

    forward_start = (
        jnp.full((tok_count, heads_here), masked_score, jnp.float32),
        jnp.zeros((tok_count, heads_here), jnp.float32),
        jnp.zeros((tok_count, heads_here, width), jnp.float32),
    )
    block_keys = lax.all_gather(latents, "leaf", axis=0, tiled=True)

    def advance(state):
        running_max, running_sum, weighted = state
        usable, logits = scores(block_keys)
        new_max = jnp.maximum(running_max, jnp.max(logits, axis=-1))
        weights = jnp.where(usable, jnp.exp(logits - new_max[..., None]), 0.0)
        weighted = jnp.einsum(
            "thk,kc->thc",
            weights.astype(jnp.bfloat16),
            block_keys,
            preferred_element_type=jnp.float32,
        )
        return (new_max, jnp.sum(weights, axis=-1), weighted)

    running_max, running_sum, weighted = advance(forward_start)
    attended = weighted / running_sum[..., None]
    log_norm = running_max + jnp.log(running_sum)
    delta = jnp.sum(grad_latent.astype(jnp.float32) * attended, axis=-1)
    backward_start = (
        jnp.zeros((tok_count, heads_here, width), jnp.float32),
        jnp.zeros((prefix_rows, width), jnp.float32),
    )
    backward_block_keys = lax.all_gather(latents, "leaf", axis=0, tiled=True)

    def advance(state):
        usable, logits = scores(backward_block_keys)
        probs = jnp.where(usable, jnp.exp(logits - log_norm[..., None]), 0.0)
        grad_weights = jnp.einsum(
            "thc,kc->thk", grad_latent, backward_block_keys, preferred_element_type=jnp.float32
        )
        grad_scores = (probs * (grad_weights - delta[..., None])).astype(jnp.bfloat16)
        query_acc = jnp.einsum(
            "thk,kc->thc", grad_scores, backward_block_keys, preferred_element_type=jnp.float32
        )
        contrib = softmax_scale * jnp.einsum(
            "thk,thc->kc", grad_scores, query_latent, preferred_element_type=jnp.float32
        )
        contrib = contrib + jnp.einsum(
            "thk,thc->kc",
            probs.astype(jnp.bfloat16),
            grad_latent,
            preferred_element_type=jnp.float32,
        )
        return (query_acc, contrib)

    query_acc, latent_grad = advance(backward_start)
    query_grad = (softmax_scale * query_acc).astype(jnp.bfloat16)
    d_queries = jnp.einsum(
        "thc,hdc->thd", query_grad, key_up_matrix, preferred_element_type=jnp.float32
    ).astype(jnp.bfloat16)
    owned_rows = lax.psum_scatter(
        latent_grad.astype(jnp.bfloat16), "leaf", scatter_dimension=0, tiled=True
    )
    d_latents = lax.psum(owned_rows, "head").astype(jnp.float32)
    return (d_queries, d_latents)


def solution(mesh):
    placed = (
        P("leaf", None),
        P("leaf", "head", None),
        P("leaf", "head", None),
        P("head", None, None),
        P("head", None, None),
        P(),
        P("leaf", None),
        P("leaf", None),
    )
    return jax.shard_map(
        on_device,
        mesh=mesh,
        in_specs=placed,
        out_specs=(P("leaf", "head", None), P("leaf", None)),
        check_vma=False,
    )
```

profile of v0, /device:TPU:4, one launch (start us, length us, event | category | flops | bytes accessed | tf_op | source)
XLA Modules:
  0.0 321.0 jit_solution(14642406166411518721)
XLA Ops:
  7.2 0.7 all-gather.2.cloned.1.call-update
  8.0 0.8 reduce-window.8
  8.8 0.1 convert_reduce_fusion
  8.9 0.7 select_reduce_fusion
  9.6 1.0 convolution_minimum_fusion.8
  10.7 0.4 convolution_minimum_fusion.7
  11.1 0.4 convolution_minimum_fusion.6
  11.4 0.4 convolution_minimum_fusion.5
  11.8 0.4 convolution_minimum_fusion.4
  12.2 0.4 convolution_minimum_fusion.3
  12.6 0.4 convolution_minimum_fusion.2
  13.0 0.4 convolution_minimum_fusion.1
  13.4 0.4 convolution_minimum_fusion
  13.8 0.3 convolution_compare_fusion
  14.0 0.1 copy.34
  14.2 0.1 broadcast_bitcast_fusion
  14.3 0.4 copy.35
  14.7 1.5 fusion.23
  16.2 2.4 fusion.24
  18.6 72.7 %all-gather.2.cloned.1.call-done = bf16[2048,512]{1,0:T(8,128)(2,1)} async-done(((bf16[64,512]{1,0:T(8,128)(2,1)}), bf16[2048,512]{1,0:T(8,128)(2,1)}) %all-gather.2.cloned.1.call-update) | async-done | bytes 2097168 | tf_op jit(solution)/shard_map/all_gather | solution.py:91
  91.3 4.5 %fusion.3 = (f32[128,8]{0,1:T(8,128)S(1)}, f32[128,8,2048]{2,0,1:T(8,128)S(1)}) fusion(pred[128,2048]{1,0:T(8,128)(4,1)S(1)} %copy.35, bf16[128,8,512]{0,2,1:T(8,128)(2,1)S(1)} %fusion.23, bf16[2048,512]{1,0:T(8,128)(2,1)} %all-gather.2.cloned.1.call-done), kind=kOutput, calls=%fused_computation.7 | convolution fusion | flops 2153774080 | bytes 11800576 | tf_op jit(solution)/shard_map/thc,kc->thk/dot_general | solution.py:58
  95.8 2.7 fusion.1
  98.5 3.3 %fusion.4 = f32[2048,512,1]{1,0,2:T(8,128)S(1)} fusion(bf16[128,8,512]{0,2,1:T(8,128)(2,1)S(1)} %copy-done.2, f32[128,8,2048]{2,0,1:T(8,128)S(1)} %get-tuple-element.9, f32[128,8]{0,1:T(8,128)S(1)} %log_add_fusion, pred[128,2048]{1,0:T(8,128)(4,1)S(1)} %copy.35), kind=kOutput, calls=%fused_computation.8 | convolution fusion | flops 2157969408 | bytes 13897728 | tf_op jit(solution)/shard_map/thk,thc->kc/dot_general | solution.py:106
  101.8 2.8 multiply_reduce_fusion
  104.6 5.5 %multiply_convert_fusion = bf16[128,8,2048]{2,0,1:T(8,128)(2,1)S(1)} fusion(f32[128,8,2048]{2,0,1:T(8,128)S(1)} %get-tuple-element.9, f32[128,8]{0,1:T(8,128)S(1)} %multiply_reduce_fusion, f32[128,8]{0,1:T(8,128)S(1)} %log_add_fusion, pred[128,2048]{1,0:T(8,128)(4,1)S(1)} %copy.35, bf16[128,8,512]{0,2,1:T(8,128)(2,1)S(1)} %copy-done.2, ...), kind=kOutput, calls=%fused_computation | convolution fusion | flops 2162163712 | bytes 15998976 | tf_op jit(solution)/shard_map/thc,kc->thk/dot_general | solution.py:96
  110.1 1.9 copy-done.4
  112.0 4.0 %fusion.6 = bf16[2048,512]{1,0:T(8,128)(2,1)} fusion(f32[2048,512,1]{1,0,2:T(8,128)S(1)} %fusion.4, bf16[128,8,2048]{2,0,1:T(8,128)(2,1)S(1)} %multiply_convert_fusion, bf16[128,8,512]{0,2,1:T(8,128)(2,1)S(1)} %fusion.23), kind=kOutput, calls=%fused_computation.10 | convolution fusion | flops 2150629376 | bytes 11534336 | tf_op jit(solution)/shard_map/thk,thc->kc/dot_general | solution.py:103
  116.1 117.2 %reduce-scatter.2.cloned.1.call-done = bf16[64,512]{1,0:T(8,128)(2,1)} async-done(((bf16[2048,512]{1,0:T(8,128)(2,1)}), bf16[64,512]{1,0:T(8,128)(2,1)}) %reduce-scatter.2.cloned.1.call-update) | async-done | bytes 65552 | tf_op jit(solution)/shard_map/reduce_scatter | solution.py:119
  233.3 5.5 %fusion.31 = bf16[128,8,128]{2,0,1:T(8,128)(2,1)S(1)} fusion(bf16[8,128,512]{2,1,0:T(8,128)(2,1)S(1)} %copy-done, bf16[128,8,2048]{2,0,1:T(8,128)(2,1)} %copy-done.4, bf16[2048,512]{1,0:T(8,128)(2,1)} %all-gather.2.cloned.1.call-done), kind=kOutput, calls=%fused_computation.42 | convolution fusion | flops 2282881024 | bytes 7602176 | tf_op jit(solution)/shard_map/thc,hdc->thd/dot_general | solution.py:116
  238.8 0.9 copy.46
  239.6 73.3 %all-reduce.2.cloned.1.call-done = bf16[64,512]{1,0:T(8,128)(2,1)} async-done(((bf16[64,512]{1,0:T(8,128)(2,1)}), bf16[64,512]{1,0:T(8,128)(2,1)}) %all-reduce.2.cloned.1.call-update) | async-done | bytes 65552 | tf_op jit(solution)/shard_map/psum | solution.py:122
  313.0 1.5 convert_element_type.57
  (16 shorter events, 0.2 us)
Async XLA Ops:
  7.2 7.6 %copy-start = (bf16[8,128,512]{2,1,0:T(8,128)(2,1)S(1)}, bf16[8,128,512]{2,1,0:T(8,128)(2,1)}, u32[]{:S(2)}) copy-start(bf16[8,128,512]{2,1,0:T(8,128)(2,1)} %param.11) | copy-start | bytes 3145732
  7.2 9.0 %copy-start.1 = (bf16[8,512,128]{2,1,0:T(8,128)(2,1)S(1)}, bf16[8,512,128]{2,1,0:T(8,128)(2,1)}, u32[]{:S(2)}) copy-start(bf16[8,512,128]{2,1,0:T(8,128)(2,1)} %param.12) | copy-start | bytes 3145732
  7.2 84.1 %all-gather.2.cloned.1.call-start = ((), (), s32[]{:S(2)}) async-start(), calls=%async_computation.1 | async-start | bytes 2162688 | tf_op jit(solution)/shard_map/all_gather | solution.py:91
  7.9 225.3 %reduce-scatter.2.cloned.1.call-start = ((), (), s32[]{:S(2)}) async-start(), calls=%async_computation.2 | async-start | bytes 2162688 | tf_op jit(solution)/shard_map/reduce_scatter | solution.py:119
  18.6 79.9 %copy-start.2 = (bf16[128,8,512]{0,2,1:T(8,128)(2,1)S(1)}, bf16[128,8,512]{0,2,1:T(8,128)(2,1)}, u32[]{:S(2)}) copy-start(bf16[128,8,512]{0,2,1:T(8,128)(2,1)} %fusion.24) | copy-start | bytes 3145732
  98.5 3.3 %copy-start.3 = (bf16[2048,512]{1,0:T(8,128)(2,1)S(1)}, bf16[2048,512]{1,0:T(8,128)(2,1)}, u32[]{:S(2)}) copy-start(bf16[2048,512]{1,0:T(8,128)(2,1)} %all-gather.2.cloned.1.call-done) | copy-start | bytes 6291460
  110.1 1.9 copy-start.4
  116.0 196.9 %all-reduce.2.cloned.1.call-start = ((), (), s32[]{:S(2)}) async-start(), calls=%async_computation.3 | async-start | bytes 131072 | tf_op jit(solution)/shard_map/psum | solution.py:122
Sparse Core Ops, SparseCore 0:
  10.8 80.4 all-gather.1
  116.2 117.0 reduce-scatter.1
  236.1 76.8 all-reduce.1
where the time goes:
time: 321 us
  waiting for transfers between devices  264 us (82%)
  matrix products  33.7 us (10%)
  between operations  14 us (4%)
  other arithmetic  5.85 us (2%)
  local copies, waits for them, and re-layouts  3.47 us (1%)
    reduce_scatter x1, waiting for transfers between devices, on_device(): lax.psum_scatter(latent_grad.astype(jnp.bfloat16), 'leaf', scatter_dimens...  117 us
    psum x1, waiting for transfers between devices, on_device(): d_latents = lax.psum(owned_rows, 'head').astype(jnp.float32)  73.3 us
    all_gather x1, waiting for transfers between devices, on_device(): backward_block_keys = lax.all_gather(latents, 'leaf', axis=0, tiled=True)  72.7 us
  transfers between devices with their start and end apart: 3, of which 3 were waited for; matrix products, arithmetic and copies ran while one was open for 5% of the time, Pallas kernels for 0%

commit v1 on v0

--- a/solution.py
+++ b/solution.py
@@ -88,7 +88,9 @@
         jnp.zeros((tok_count, heads_here, width), jnp.float32),
         jnp.zeros((prefix_rows, width), jnp.float32),
     )
-    backward_block_keys = lax.all_gather(latents, "leaf", axis=0, tiled=True)
+    backward_block_keys = jnp.concatenate(
+        lax.all_to_all(jnp.stack([latents] * lax.axis_size("leaf")), "leaf", 0, 0), axis=0
+    )
 
     def advance(state):
         usable, logits = scores(backward_block_keys)

time: 321 us -> 334 us (1.040)
  starting transfers between devices: 0.12 us -> 11.8 us
  waiting for transfers between devices: 264 us -> 256 us
  matrix products: 33.7 us -> 39.1 us
  local copies, waits for them, and re-layouts: 3.47 us -> 8.12 us
    all_to_all x0 -> x1, starting transfers between devices: none -> 11.7 us  [on_device(): lax.all_to_all(jnp.stack([latents] * lax.axis_size('leaf')), 'leaf', 0, 0)]
    all_gather x1, waiting for transfers between devices: 72.7 us -> 64.4 us  [on_device(): block_keys = lax.all_gather(latents, 'leaf', axis=0, tiled=True)]
    dot_general x1 -> x2, matrix products: 4.49 us -> 8.58 us  [scores(): jnp.einsum('thc,kc->thk', query_latent, block_keys, preferred_element_typ...]
  transfers between devices with their start and end apart: 3 -> 4, of which waited for: 3 -> 3; matrix products, arithmetic and copies ran while one was open for 5% -> 8% of each run, Pallas kernels for 0% -> 0%
where the time goes in v1:
time: 334 us
  waiting for transfers between devices  256 us (77%)
  matrix products  39.1 us (12%)
  between operations  14 us (4%)
  starting transfers between devices  11.8 us (4%)
  local copies, waits for them, and re-layouts  8.12 us (2%)
  other arithmetic  4.55 us (1%)
    reduce_scatter x1, waiting for transfers between devices, on_device(): lax.psum_scatter(latent_grad.astype(jnp.bfloat16), 'leaf', scatter_dimens...  117 us
    psum x1, waiting for transfers between devices, on_device(): d_latents = lax.psum(owned_rows, 'head').astype(jnp.float32)  74 us
    all_gather x1, waiting for transfers between devices, on_device(): block_keys = lax.all_gather(latents, 'leaf', axis=0, tiled=True)  64.4 us
    all_to_all x1, starting transfers between devices, on_device(): lax.all_to_all(jnp.stack([latents] * lax.axis_size('leaf')), 'leaf', 0, 0)  11.7 us
    dot_general x2, matrix products, scores(): jnp.einsum('thc,kc->thk', query_latent, block_keys, preferred_element_typ...  8.58 us
  transfers between devices with their start and end apart: 4, of which 3 were waited for; matrix products, arithmetic and copies ran while one was open for 8% of the time, Pallas kernels for 0%

profile of v1, /device:TPU:4, one launch (start us, length us, event | category | flops | bytes accessed | tf_op | source)
XLA Modules:
  0.0 334.1 jit_solution(7294920062852360928)
XLA Ops:
  7.2 0.7 all-gather.2.cloned.1.call-update
  7.9 2.4 stack.2
  10.4 11.7 %all-to-all-start = ((bf16[32,64,512]{2,1,0:T(8,128)(2,1)}), bf16[32,64,512]{2,1,0:T(8,128)(2,1)S(1)}, u32[]{:S(2)}, u32[]{:S(2)}) async-start(bf16[32,64,512]{2,1,0:T(8,128)(2,1)} %stack.2), calls=%async_computation | async-start | bytes 4194304 | tf_op jit(solution)/shard_map/all_to_all | solution.py:92
  22.4 0.3 convolution_minimum_fusion.8
  22.7 0.4 convolution_minimum_fusion.7
  23.1 0.4 convolution_minimum_fusion.6
  23.5 0.4 convolution_minimum_fusion.5
  23.9 0.4 convolution_minimum_fusion.4
  24.4 0.4 convolution_minimum_fusion.3
  24.8 0.4 convolution_minimum_fusion.2
  25.2 0.4 convolution_minimum_fusion.1
  25.5 0.4 convolution_minimum_fusion
  25.9 0.3 convolution_compare_fusion
  26.3 0.8 broadcast_bitcast_fusion
  27.2 1.4 copy.37
  28.5 2.5 fusion.18
  31.0 2.7 fusion.19
  33.7 64.4 %all-gather.2.cloned.1.call-done = bf16[2048,512]{1,0:T(8,128)(2,1)} async-done(((bf16[64,512]{1,0:T(8,128)(2,1)}), bf16[2048,512]{1,0:T(8,128)(2,1)}) %all-gather.2.cloned.1.call-update) | async-done | bytes 2097168 | tf_op jit(solution)/shard_map/all_gather | solution.py:68
  98.0 4.8 %fusion = (f32[128,8]{0,1:T(8,128)S(1)}, f32[128,8,2048]{2,0,1:T(8,128)S(1)}) fusion(pred[128,2048]{1,0:T(8,128)(4,1)S(1)} %copy.37, bf16[128,8,512]{0,2,1:T(8,128)(2,1)} %fusion.18, bf16[2048,512]{1,0:T(8,128)(2,1)} %all-gather.2.cloned.1.call-done), kind=kOutput, calls=%fused_computation.4 | convolution fusion | flops 2153774080 | bytes 11800576 | tf_op jit(solution)/shard_map/thc,kc->thk/dot_general | solution.py:58
  102.9 2.7 fusion.2
  105.6 0.5 copy-done.1
  106.1 3.8 %fusion.41 = f32[128,8,2048]{2,0,1:T(8,128)S(1)} fusion(bf16[128,8,512]{0,2,1:T(8,128)(2,1)} %fusion.18, bf16[2048,512,1]{1,0,2:T(8,128)(2,1)S(1)} %bitcast.63), kind=kOutput, calls=%fused_computation.64 | convolution fusion | flops 2147483648 | bytes 11534336 | tf_op jit(solution)/shard_map/thc,kc->thk/dot_general | solution.py:58
  109.9 5.0 %fusion.4 = f32[2048,512,1]{1,0,2:T(8,128)} fusion(bf16[128,8,512]{0,2,1:T(8,128)(2,1)S(1)} %copy-done.3, f32[128,8,2048]{2,0,1:T(8,128)S(1)} %fusion.41, f32[128,8]{0,1:T(8,128)S(1)} %log_add_fusion, pred[128,2048]{1,0:T(8,128)(4,1)S(1)} %copy.37), kind=kOutput, calls=%fused_computation.8 | convolution fusion | flops 2157969408 | bytes 13897728 | tf_op jit(solution)/shard_map/thk,thc->kc/dot_general | solution.py:108
  115.0 2.8 multiply_reduce_fusion
  117.8 5.4 %multiply_convert_fusion = bf16[128,8,2048]{2,0,1:T(8,128)(2,1)S(1)} fusion(f32[128,8,2048]{2,0,1:T(8,128)S(1)} %fusion.41, f32[128,8]{0,1:T(8,128)S(1)} %multiply_reduce_fusion, f32[128,8]{0,1:T(8,128)S(1)} %log_add_fusion, pred[128,2048]{1,0:T(8,128)(4,1)S(1)} %copy.37, bf16[128,8,512]{0,2,1:T(8,128)(2,1)S(1)} %copy-done.3, ...), kind=kOutput, calls=%fused_computation | convolution fusion | flops 2162163712 | bytes 15998976 | tf_op jit(solution)/shard_map/thc,kc->thk/dot_general | solution.py:98
  123.2 1.9 copy-done.8
  125.2 3.7 %fusion.6 = bf16[2048,512]{1,0:T(8,128)(2,1)} fusion(f32[2048,512,1]{1,0,2:T(8,128)S(1)} %copy-done.9, bf16[128,8,2048]{2,0,1:T(8,128)(2,1)S(1)} %multiply_convert_fusion, bf16[128,8,512]{0,2,1:T(8,128)(2,1)S(1)} %copy-done.2), kind=kOutput, calls=%fused_computation.10 | convolution fusion | flops 2150629376 | bytes 11534336 | tf_op jit(solution)/shard_map/thk,thc->kc/dot_general | solution.py:105
  129.0 117.4 %reduce-scatter.2.cloned.1.call-done = bf16[64,512]{1,0:T(8,128)(2,1)} async-done(((bf16[2048,512]{1,0:T(8,128)(2,1)}), bf16[64,512]{1,0:T(8,128)(2,1)}) %reduce-scatter.2.cloned.1.call-update) | async-done | bytes 65552 | tf_op jit(solution)/shard_map/reduce_scatter | solution.py:121
  246.4 4.8 %fusion.22 = bf16[128,8,128]{2,0,1:T(8,128)(2,1)S(1)} fusion(bf16[8,128,512]{2,1,0:T(8,128)(2,1)S(1)} %copy-done, bf16[128,8,2048]{2,0,1:T(8,128)(2,1)} %copy-done.8, bf16[2048,512,1]{1,0,2:T(8,128)(2,1)S(1)} %bitcast.65), kind=kOutput, calls=%fused_computation.39 | convolution fusion | flops 2282881024 | bytes 7602176 | tf_op jit(solution)/shard_map/thc,hdc->thd/dot_general | solution.py:118
  251.2 0.9 copy.49
  252.1 74.0 %all-reduce.2.cloned.1.call-done = bf16[64,512]{1,0:T(8,128)(2,1)} async-done(((bf16[64,512]{1,0:T(8,128)(2,1)}), bf16[64,512]{1,0:T(8,128)(2,1)}) %all-reduce.2.cloned.1.call-update) | async-done | bytes 65552 | tf_op jit(solution)/shard_map/psum | solution.py:124
  326.1 1.5 convert_element_type.57
  (35 shorter events, 0.7 us)
Async XLA Ops:
  7.2 21.4 %copy-start = (bf16[8,128,512]{2,1,0:T(8,128)(2,1)S(1)}, bf16[8,128,512]{2,1,0:T(8,128)(2,1)}, u32[]{:S(2)}) copy-start(bf16[8,128,512]{2,1,0:T(8,128)(2,1)} %param.11) | copy-start | bytes 3145732
  7.2 15.0 %copy-start.6 = (s32[1,8]{1,0:T(1,128)S(1)}, s32[1,8]{1,0:T(1,128)}, u32[]{:S(2)}) copy-start(s32[1,8]{1,0:T(1,128)} %param.15) | copy-start | bytes 100
  7.2 15.3 %copy-start.5 = (s32[256]{0:T(256)S(1)}, s32[256]{0:T(256)}, u32[]{:S(2)}) copy-start(s32[256]{0:T(256)} %param.13) | copy-start | bytes 3076
  7.2 90.8 %all-gather.2.cloned.1.call-start = ((), (), s32[]{:S(2)}) async-start(), calls=%async_computation.2 | async-start | bytes 2162688 | tf_op jit(solution)/shard_map/all_gather | solution.py:68
  10.4 13.9 %copy-start.7 = (s32[1,8]{1,0:T(1,128)S(1)}, s32[1,8]{1,0:T(1,128)}, u32[]{:S(2)}) copy-start(s32[1,8]{1,0:T(1,128)} %param.14) | copy-start | bytes 100
  10.4 95.7 %all-to-all-start = ((bf16[32,64,512]{2,1,0:T(8,128)(2,1)}), bf16[32,64,512]{2,1,0:T(8,128)(2,1)S(1)}, u32[]{:S(2)}, u32[]{:S(2)}) async-start(bf16[32,64,512]{2,1,0:T(8,128)(2,1)} %stack.2), calls=%async_computation | async-start | bytes 4194304 | tf_op jit(solution)/shard_map/all_to_all | solution.py:92
  22.1 224.3 %reduce-scatter.2.cloned.1.call-start = ((), (), s32[]{:S(2)}) async-start(), calls=%async_computation.3 | async-start | bytes 2162688 | tf_op jit(solution)/shard_map/reduce_scatter | solution.py:121
  102.8 3.2 copy-start.1
  106.1 3.8 %copy-start.3 = (bf16[128,8,512]{0,2,1:T(8,128)(2,1)S(1)}, bf16[128,8,512]{0,2,1:T(8,128)(2,1)}, u32[]{:S(2)}) copy-start(bf16[128,8,512]{0,2,1:T(8,128)(2,1)} %fusion.19) | copy-start | bytes 3145732
  106.1 8.9 %slice-start = ((s8[8388608]{0:T(1024)(128)(4,1)}), s8[4194304]{0:T(1024)(128)(4,1)S(1)}, s32[]{:S(2)}) async-start(s8[8388608]{0:T(1024)(128)(4,1)} %bitcast.61), calls=%async_computation.5 | async-start | bytes 8388608
  109.9 5.1 %slice-start.1 = ((s8[8388608]{0:T(1024)(128)(4,1)}), s8[4194304]{0:T(1024)(128)(4,1)S(1)}, s32[]{:S(2)}) async-start(s8[8388608]{0:T(1024)(128)(4,1)} %bitcast.61), calls=%async_computation.6 | async-start | bytes 8388608
  109.9 5.1 %copy-start.4 = (bf16[2048,512]{1,0:T(8,128)(2,1)S(1)}, bf16[2048,512]{1,0:T(8,128)(2,1)}, u32[]{:S(2)}) copy-start(bf16[2048,512]{1,0:T(8,128)(2,1)} %all-gather.2.cloned.1.call-done) | copy-start | bytes 6291460
  117.8 7.4 %copy-start.2 = (bf16[128,8,512]{0,2,1:T(8,128)(2,1)S(1)}, bf16[128,8,512]{0,2,1:T(8,128)(2,1)}, u32[]{:S(2)}) copy-start(bf16[128,8,512]{0,2,1:T(8,128)(2,1)} %fusion.18) | copy-start | bytes 3145732
  117.8 7.4 %copy-start.9 = (f32[2048,512,1]{1,0,2:T(8,128)S(1)}, f32[2048,512,1]{1,0,2:T(8,128)}, u32[]{:S(2)}) copy-start(f32[2048,512,1]{1,0,2:T(8,128)} %fusion.4) | copy-start | bytes 12582916
  123.2 1.9 copy-start.8
  128.9 197.1 %all-reduce.2.cloned.1.call-start = ((), (), s32[]{:S(2)}) async-start(), calls=%async_computation.4 | async-start | bytes 131072 | tf_op jit(solution)/shard_map/psum | solution.py:124
Sparse Core Ops, SparseCore 0:
  10.8 87.1 all-gather.1
  129.1 117.2 reduce-scatter.1
  249.2 76.8 all-reduce.1
